TPU v7x, 512 devices: a whole 4x8x8 slice. The times are simulated.
512 devices in a mesh: dp: 64 (over y, z_hi, core), tensor: 8 (over x, z_lo).
Axes of the slice: x: 4, y: 8, z: 8 (z_hi: 4, z_lo: 2; z = z_hi * 2 + z_lo), core: 2. Of those that a mesh axis runs over, the one named last changes fastest.
Arguments:
- inputs: float32 [16384, 1024], P('dp', 'tensor'), may hold values from -16 to 16
- cotangent: float32 [16384, 1024], P('dp', 'tensor'), may hold values from -0.12 to 0.12
- gate_weight: float32 [1024, 4096], P('dp', 'tensor'), may hold values from -0.1875 to 0.1875
- up_weight: float32 [1024, 4096], P('dp', 'tensor'), may hold values from -0.1875 to 0.1875
- down_weight: float32 [1024, 4096], P('dp', 'tensor'), may hold values from -0.09375 to 0.09375
- gate_first: float32 [1024, 4096], P('dp', 'tensor'), may hold values from -6 to 6
- gate_second: float32 [1024, 4096], P('dp', 'tensor'), may hold values from 0.5 to 4
- up_first: float32 [1024, 4096], P('dp', 'tensor'), may hold values from -6 to 6
- up_second: float32 [1024, 4096], P('dp', 'tensor'), may hold values from 0.5 to 4
Outputs:
- gate_new: float32 [1024, 4096], P('dp', 'tensor')
- gate_first_new: float32 [1024, 4096], P('dp', 'tensor')
- gate_second_new: float32 [1024, 4096], P('dp', 'tensor')
- up_new: float32 [1024, 4096], P('dp', 'tensor')
- up_first_new: float32 [1024, 4096], P('dp', 'tensor')
- up_second_new: float32 [1024, 4096], P('dp', 'tensor')
All inputs are finite; a program needn't handle non-finite values.
Results may differ from a plain program's by a relative error of at most 0.00005.
Values sent between devices are 32-bit elements; how exact they have to be, the bound alone decides.
A program may use at most 64 MiB of HBM per device.

v0:
```python
import jax
import jax.numpy as jnp
from jax import lax
from jax.sharding import PartitionSpec as P

STEP = 100


def adam_update(weight, first, second, grad):
    first_new = 0.9 * first + 0.1 * grad
    second_new = 0.95 * second + 0.05 * grad * grad
    first_hat = first_new / (1.0 - 0.9**STEP)
    second_hat = second_new / (1.0 - 0.95**STEP)
    weight_new = weight - 0.003 * first_hat / (jnp.sqrt(second_hat) + 1e-08)
    return (weight_new, first_new, second_new)


def contract(left, piece):
    return jnp.dot(left, piece, precision=lax.Precision.HIGHEST, preferred_element_type=jnp.float32)


def local(
    inputs,
    cotangent,
    gate_weight,
    up_weight,
    down_weight,
    gate_first,
    gate_second,
    up_first,
    up_second,
):
    rows_full, cot_full = (
        lax.all_gather(inputs, "tensor", axis=1, tiled=True),
        lax.all_gather(cotangent, "tensor", axis=1, tiled=True),
    )
    gate_sum = contract(rows_full, lax.all_gather(gate_weight, "dp", axis=0, tiled=True))
    lift_sum = contract(rows_full, lax.all_gather(up_weight, "dp", axis=0, tiled=True))
    back_sum = contract(cot_full, lax.all_gather(down_weight, "dp", axis=0, tiled=True))
    sigmoid_gate = jax.nn.sigmoid(gate_sum)
    gate_rows = back_sum * lift_sum * sigmoid_gate * (1.0 + gate_sum * (1.0 - sigmoid_gate))
    lift_rows = back_sum * gate_sum * sigmoid_gate

    def make_term(grad_rows):
        return lax.dot_general(
            rows_full,
            grad_rows,
            (((0,), (0,)), ((), ())),
            precision=lax.Precision.HIGHEST,
            preferred_element_type=jnp.float32,
        )

    gate_grad = lax.psum_scatter(make_term(gate_rows), "dp", scatter_dimension=0, tiled=True)
    lift_grad = lax.psum_scatter(make_term(lift_rows), "dp", scatter_dimension=0, tiled=True)
    gate_new, gate_first_new, gate_second_new = adam_update(
        gate_weight, gate_first, gate_second, gate_grad
    )
    up_new, up_first_new, up_second_new = adam_update(up_weight, up_first, up_second, lift_grad)
    return (gate_new, gate_first_new, gate_second_new, up_new, up_first_new, up_second_new)


def solution(mesh):
    in_specs = (
        P("dp", "tensor"),
        P("dp", "tensor"),
        P("dp", "tensor"),
        P("dp", "tensor"),
        P("dp", "tensor"),
        P("dp", "tensor"),
        P("dp", "tensor"),
        P("dp", "tensor"),
        P("dp", "tensor"),
    )
    out_specs = (
        P("dp", "tensor"),
        P("dp", "tensor"),
        P("dp", "tensor"),
        P("dp", "tensor"),
        P("dp", "tensor"),
        P("dp", "tensor"),
    )
    return jax.shard_map(local, mesh=mesh, in_specs=in_specs, out_specs=out_specs, check_vma=False)
```

profile of v0, /device:TPU:2, one launch (start us, length us, event | category | flops | bytes accessed | tf_op | source)
XLA Modules:
  0.0 683.1 jit_solution(2127603420906008118)
XLA Ops:
  7.2 0.0 all-gather.6.cloned.1.call-start
  7.2 0.7 all-gather.6.cloned.1.call-update
  7.9 0.0 all-gather.8.cloned.1.call-start
  7.9 0.7 all-gather.8.cloned.1.call-update
  8.6 0.0 all-gather.10.cloned.1.call-start
  8.7 0.7 all-gather.10.cloned.1.call-update
  9.4 0.0 all-gather.14.cloned.1.call-start
  9.4 0.5 all-gather.14.cloned.1.call-update
  10.0 0.0 all-gather.12.cloned.1.call-start
  10.0 0.5 all-gather.12.cloned.1.call-update
  10.5 0.0 reduce-scatter.9.cloned.1.call-start
  10.6 49.5 %all-gather.6.cloned.1.call-done = f32[256,1024]{1,0:T(8,128)} async-done(((f32[256,128]{1,0:T(8,128)}), f32[256,1024]{1,0:T(8,128)}) %all-gather.6.cloned.1.call-update) | async-done | bytes 1048592 | tf_op jit(solution)/shard_map/all_gather | solution.py:35
  60.1 89.3 %all-gather.8.cloned.1.call-done = f32[1024,512]{1,0:T(8,128)} async-done(((f32[16,512]{1,0:T(8,128)}), f32[1024,512]{1,0:T(8,128)}) %all-gather.8.cloned.1.call-update) | async-done | bytes 2097168 | tf_op jit(solution)/shard_map/all_gather | solution.py:39
  149.4 4.7 fusion.10
  154.1 39.5 %all-gather.10.cloned.1.call-done = f32[256,1024]{1,0:T(8,128)} async-done(((f32[256,128]{1,0:T(8,128)}), f32[256,1024]{1,0:T(8,128)}) %all-gather.10.cloned.1.call-update) | async-done | bytes 1048592 | tf_op jit(solution)/shard_map/all_gather | solution.py:34
  193.7 0.0 copy-start
  193.7 89.2 %all-gather.14.cloned.1.call-done = f32[1024,512]{1,0:T(8,128)} async-done(((f32[16,512]{1,0:T(8,128)}), f32[1024,512]{1,0:T(8,128)}) %all-gather.14.cloned.1.call-update) | async-done | bytes 2097168 | tf_op jit(solution)/shard_map/all_gather | solution.py:37
  282.8 0.0 copy-start.1
  282.8 3.9 fusion.11
  286.7 0.0 copy-start.3
  286.7 0.8 copy-done.3
  287.6 0.0 copy-done
  287.6 0.0 copy-done.1
  287.6 2.0 convolution_bitcast_fusion
  289.5 1.8 copy.55
  291.3 0.0 copy-start.2
  291.3 0.0 copy-start.4
  291.3 0.0 reduce-scatter.9.cloned.1.call-update
  291.4 0.0 reduce-scatter.7.cloned.1.call-start
  291.4 76.3 %all-gather.12.cloned.1.call-done = f32[1024,512]{1,0:T(8,128)} async-done(((f32[16,512]{1,0:T(8,128)}), f32[1024,512]{1,0:T(8,128)}) %all-gather.12.cloned.1.call-update) | async-done | bytes 2097168 | tf_op jit(solution)/shard_map/all_gather | solution.py:38
  367.7 0.0 copy-done.2
  367.7 0.0 copy-done.4
  367.7 3.6 fusion.1
  371.4 1.9 convolution_bitcast_fusion.1
  373.2 1.8 copy.53
  375.1 0.0 copy-start.5
  375.1 0.0 copy-start.7
  375.1 0.0 copy-start.8
  375.1 0.0 copy-start.6
  375.1 0.0 copy-start.9
  375.1 0.0 copy-start.10
  375.1 0.0 reduce-scatter.7.cloned.1.call-update
  375.1 146.2 %reduce-scatter.9.cloned.1.call-done = f32[16,512]{1,0:T(8,128)} async-done(((f32[1024,512]{1,0:T(8,128)}), f32[16,512]{1,0:T(8,128)}) %reduce-scatter.9.cloned.1.call-update) | async-done | bytes 32784 | tf_op jit(solution)/shard_map/reduce_scatter | solution.py:54
  521.4 0.0 copy-done.5
  521.4 0.0 copy-done.7
  521.4 0.0 copy-done.8
  521.4 1.4 divide_subtract_fusion
  522.8 152.1 %reduce-scatter.7.cloned.1.call-done = f32[16,512]{1,0:T(8,128)} async-done(((f32[1024,512]{1,0:T(8,128)}), f32[16,512]{1,0:T(8,128)}) %reduce-scatter.7.cloned.1.call-update) | async-done | bytes 32784 | tf_op jit(solution)/shard_map/reduce_scatter | solution.py:53
  674.9 0.0 copy-done.6
  674.9 0.0 copy-done.9
  674.9 0.0 copy-done.10
  674.9 1.4 divide_subtract_fusion.1
Async XLA Ops:
  7.2 52.9 %all-gather.6.cloned.1.call-start = ((), (), s32[]{:S(2)}) async-start(), calls=%async_computation.2 | async-start | bytes 1179648 | tf_op jit(solution)/shard_map/all_gather | solution.py:35
  7.9 141.5 %all-gather.8.cloned.1.call-start = ((), (), s32[]{:S(2)}) async-start(), calls=%async_computation.3 | async-start | bytes 2129920 | tf_op jit(solution)/shard_map/all_gather | solution.py:39
  8.6 185.0 %all-gather.10.cloned.1.call-start = ((), (), s32[]{:S(2)}) async-start(), calls=%async_computation.4 | async-start | bytes 1179648 | tf_op jit(solution)/shard_map/all_gather | solution.py:34
  9.4 273.4 %all-gather.14.cloned.1.call-start = ((), (), s32[]{:S(2)}) async-start(), calls=%async_computation.6 | async-start | bytes 2129920 | tf_op jit(solution)/shard_map/all_gather | solution.py:37
  10.0 357.8 %all-gather.12.cloned.1.call-start = ((), (), s32[]{:S(2)}) async-start(), calls=%async_computation.5 | async-start | bytes 2129920 | tf_op jit(solution)/shard_map/all_gather | solution.py:38
  10.5 510.8 %reduce-scatter.9.cloned.1.call-start = ((), (), s32[]{:S(2)}) async-start(), calls=%async_computation.8 | async-start | bytes 2129920 | tf_op jit(solution)/shard_map/reduce_scatter | solution.py:54
  193.7 93.9 %copy-start = (f32[256,1024]{1,0:T(8,128)S(1)}, f32[256,1024]{1,0:T(8,128)}, u32[]{:S(2)}) copy-start(f32[256,1024]{1,0:T(8,128)} %all-gather.10.cloned.1.call-done) | copy-start | bytes 3145732
  282.8 4.7 copy-start.1
  286.7 0.8 copy-start.3
  291.3 76.4 %copy-start.2 = (f32[256,512]{1,0:T(8,128)S(1)}, f32[256,512]{1,0:T(8,128)}, u32[]{:S(2)}) copy-start(f32[256,512]{1,0:T(8,128)} %fusion.10) | copy-start | bytes 1572868
  291.3 76.4 %copy-start.4 = (f32[256,512]{1,0:T(8,128)S(1)}, f32[256,512]{1,0:T(8,128)}, u32[]{:S(2)}) copy-start(f32[256,512]{1,0:T(8,128)} %copy-done.3) | copy-start | bytes 1572868
  291.4 383.5 %reduce-scatter.7.cloned.1.call-start = ((), (), s32[]{:S(2)}) async-start(), calls=%async_computation.7 | async-start | bytes 2129920 | tf_op jit(solution)/shard_map/reduce_scatter | solution.py:53
  375.1 146.3 %copy-start.5 = (f32[16,512]{1,0:T(8,128)S(1)}, f32[16,512]{1,0:T(8,128)}, u32[]{:S(2)}) copy-start(f32[16,512]{1,0:T(8,128)} %param.12) | copy-start | bytes 98308
  375.1 146.3 %copy-start.7 = (f32[16,512]{1,0:T(8,128)S(1)}, f32[16,512]{1,0:T(8,128)}, u32[]{:S(2)}) copy-start(f32[16,512]{1,0:T(8,128)} %param.16) | copy-start | bytes 98308
  375.1 146.3 %copy-start.8 = (f32[16,512]{1,0:T(8,128)S(1)}, f32[16,512]{1,0:T(8,128)}, u32[]{:S(2)}) copy-start(f32[16,512]{1,0:T(8,128)} %param.17) | copy-start | bytes 98308
  375.1 299.8 %copy-start.6 = (f32[16,512]{1,0:T(8,128)S(1)}, f32[16,512]{1,0:T(8,128)}, u32[]{:S(2)}) copy-start(f32[16,512]{1,0:T(8,128)} %param.11) | copy-start | bytes 98308
  375.1 299.8 %copy-start.9 = (f32[16,512]{1,0:T(8,128)S(1)}, f32[16,512]{1,0:T(8,128)}, u32[]{:S(2)}) copy-start(f32[16,512]{1,0:T(8,128)} %param.14) | copy-start | bytes 98308
  375.1 299.8 %copy-start.10 = (f32[16,512]{1,0:T(8,128)S(1)}, f32[16,512]{1,0:T(8,128)}, u32[]{:S(2)}) copy-start(f32[16,512]{1,0:T(8,128)} %param.15) | copy-start | bytes 98308
Sparse Core Ops, SparseCore 0:
  10.0 50.0 all-gather.5
  63.4 85.9 all-gather.7
  151.4 42.1 all-gather.9
  196.8 85.9 all-gather.13
  286.0 81.6 all-gather.11
  372.2 149.1 reduce-scatter.8
  526.0 148.8 reduce-scatter.6
where the time goes:
time: 683 us
  waiting for transfers between devices  645 us (94%)
  matrix products  16.1 us (2%)
  between operations  14.2 us (2%)
    reduce_scatter x1, waiting for transfers between devices, local(): lax.psum_scatter(make_term(gate_rows), 'dp', scatter_dimension=0, tiled=T...  152 us
    reduce_scatter x1, waiting for transfers between devices, local(): lax.psum_scatter(make_term(lift_rows), 'dp', scatter_dimension=0, tiled=T...  146 us
    all_gather x1, waiting for transfers between devices, local(): lax.all_gather(down_weight, 'dp', axis=0, tiled=True)  89.3 us
    all_gather x1, waiting for transfers between devices, local(): lax.all_gather(gate_weight, 'dp', axis=0, tiled=True)  89.2 us
    all_gather x1, waiting for transfers between devices, local(): lax.all_gather(up_weight, 'dp', axis=0, tiled=True)  76.3 us
    all_gather x1, waiting for transfers between devices, local(): lax.all_gather(cotangent, 'tensor', axis=1, tiled=True)  49.5 us
    all_gather x1, waiting for transfers between devices, local(): lax.all_gather(inputs, 'tensor', axis=1, tiled=True)  39.5 us
  transfers between devices with their start and end apart: 7, of which 7 were waited for; matrix products, arithmetic and copies ran while one was open for 3% of the time, Pallas kernels for 0%

commit v1 on v0

--- a/solution.py
+++ b/solution.py
@@ -31,7 +31,9 @@
     up_second,
 ):
     rows_full, cot_full = (
-        lax.all_gather(inputs, "tensor", axis=1, tiled=True),
+        jnp.concatenate(
+            lax.all_to_all(jnp.stack([inputs] * lax.axis_size("tensor")), "tensor", 0, 0), axis=1
+        ),
         lax.all_gather(cotangent, "tensor", axis=1, tiled=True),
     )
     gate_sum = contract(rows_full, lax.all_gather(gate_weight, "dp", axis=0, tiled=True))

time: 683 us -> 640 us (0.937)
  waiting for transfers between devices: 645 us -> 578 us
  blocking collectives: 0 us -> 20.4 us
    all_gather x1 -> x0, waiting for transfers between devices: 39.5 us -> none  [local(): lax.all_gather(inputs, 'tensor', axis=1, tiled=True)]
    all_to_all x0 -> x1, blocking collectives: none -> 20.4 us  [local(): lax.all_to_all(jnp.stack([inputs] * lax.axis_size('tensor')), 'tensor', 0...]
    all_gather x1, waiting for transfers between devices: 89.2 us -> 69.4 us  [local(): lax.all_gather(gate_weight, 'dp', axis=0, tiled=True)]
    reduce_scatter x1, waiting for transfers between devices: 152 us -> 142 us  [local(): lax.psum_scatter(make_term(gate_rows), 'dp', scatter_dimension=0, tiled=T...]
    all_gather x1, waiting for transfers between devices: 49.5 us -> 40.7 us  [local(): lax.all_gather(cotangent, 'tensor', axis=1, tiled=True)]
  transfers between devices with their start and end apart: 7 -> 6, of which waited for: 7 -> 6; matrix products, arithmetic and copies ran while one was open for 3% -> 3% of each run, Pallas kernels for 0% -> 0%
where the time goes in v1:
time: 640 us; the launch traced here: 639 us
  waiting for transfers between devices  578 us (90%)
  blocking collectives  20.4 us (3%)
  matrix products  19.3 us (3%)
  between operations  14.2 us (2%)
    reduce_scatter x1, waiting for transfers between devices, local(): lax.psum_scatter(make_term(lift_rows), 'dp', scatter_dimension=0, tiled=T...  152 us
    reduce_scatter x1, waiting for transfers between devices, local(): lax.psum_scatter(make_term(gate_rows), 'dp', scatter_dimension=0, tiled=T...  142 us
    all_gather x1, waiting for transfers between devices, local(): lax.all_gather(down_weight, 'dp', axis=0, tiled=True)  89.3 us
    all_gather x1, waiting for transfers between devices, local(): lax.all_gather(up_weight, 'dp', axis=0, tiled=True)  81 us
    all_gather x1, waiting for transfers between devices, local(): lax.all_gather(gate_weight, 'dp', axis=0, tiled=True)  69.4 us
    all_gather x1, waiting for transfers between devices, local(): lax.all_gather(cotangent, 'tensor', axis=1, tiled=True)  40.7 us
    all_to_all x1, blocking collectives, local(): lax.all_to_all(jnp.stack([inputs] * lax.axis_size('tensor')), 'tensor', 0...  20.4 us
  transfers between devices with their start and end apart: 6, of which 6 were waited for; matrix products, arithmetic and copies ran while one was open for 3% of the time, Pallas kernels for 0%

profile of v1, /device:TPU:2, one launch (start us, length us, event | category | flops | bytes accessed | tf_op | source)
XLA Modules:
  0.0 639.4 jit_solution(4147681388615940851)
XLA Ops:
  7.2 0.0 all-gather.11.cloned.1.call-start
  7.2 0.7 all-gather.11.cloned.1.call-update
  7.9 0.0 all-gather.5.cloned.1.call-start
  7.9 0.7 all-gather.5.cloned.1.call-update
  8.6 0.0 all-gather.7.cloned.1.call-start
  8.7 0.7 all-gather.7.cloned.1.call-update
  9.4 0.0 all-gather.9.cloned.1.call-start
  9.4 0.5 all-gather.9.cloned.1.call-update
  10.0 0.0 reduce-scatter.7.cloned.1.call-start
  10.0 1.0 copy.65
  11.0 0.1 stack.2
  11.1 20.4 %all_to_all.5 = f32[8,256,128]{1,2,0:T(8,128)S(1)} all-to-all(f32[8,256,128]{1,2,0:T(8,128)S(1)} %stack.2), channel_id=1, replica_groups=mesh['dp'=64,'tensor'=8] {'tensor'}, dimensions={0} | all-to-all | bytes 2097152 | tf_op jit(solution)/shard_map/all_to_all | solution.py:35
  31.5 69.4 %all-gather.11.cloned.1.call-done = f32[1024,512]{1,0:T(8,128)} async-done(((f32[16,512]{1,0:T(8,128)}), f32[1024,512]{1,0:T(8,128)}) %all-gather.11.cloned.1.call-update) | async-done | bytes 2097168 | tf_op jit(solution)/shard_map/all_gather | solution.py:39
  100.9 3.5 fusion.11
  104.4 0.0 copy-start
  104.4 40.7 %all-gather.5.cloned.1.call-done = f32[256,1024]{1,0:T(8,128)} async-done(((f32[256,128]{1,0:T(8,128)}), f32[256,1024]{1,0:T(8,128)}) %all-gather.5.cloned.1.call-update) | async-done | bytes 1048592 | tf_op jit(solution)/shard_map/all_gather | solution.py:37
  145.2 89.3 %all-gather.7.cloned.1.call-done = f32[1024,512]{1,0:T(8,128)} async-done(((f32[16,512]{1,0:T(8,128)}), f32[1024,512]{1,0:T(8,128)}) %all-gather.7.cloned.1.call-update) | async-done | bytes 2097168 | tf_op jit(solution)/shard_map/all_gather | solution.py:41
  234.5 3.8 fusion.10
  238.3 0.0 copy-start.1
  238.3 81.0 %all-gather.9.cloned.1.call-done = f32[1024,512]{1,0:T(8,128)} async-done(((f32[16,512]{1,0:T(8,128)}), f32[1024,512]{1,0:T(8,128)}) %all-gather.9.cloned.1.call-update) | async-done | bytes 2097168 | tf_op jit(solution)/shard_map/all_gather | solution.py:40
  319.4 0.0 copy-done
  319.4 0.0 copy-done.1
  319.4 3.6 fusion.1
  323.0 3.6 convolution_bitcast_fusion.1
  326.6 1.8 copy.72
  328.4 0.0 reduce-scatter.7.cloned.1.call-update
  328.4 0.2 reduce-scatter.9.cloned.1.call-start
  328.6 4.7 convolution_bitcast_fusion
  333.4 1.8 copy.74
  335.2 0.0 copy-start.2
  335.2 0.0 copy-start.4
  335.2 0.0 copy-start.5
  335.2 0.0 copy-start.3
  335.2 0.0 copy-start.6
  335.2 0.0 copy-start.7
  335.2 0.0 reduce-scatter.9.cloned.1.call-update
  335.2 142.5 %reduce-scatter.7.cloned.1.call-done = f32[16,512]{1,0:T(8,128)} async-done(((f32[1024,512]{1,0:T(8,128)}), f32[16,512]{1,0:T(8,128)}) %reduce-scatter.7.cloned.1.call-update) | async-done | bytes 32784 | tf_op jit(solution)/shard_map/reduce_scatter | solution.py:55
  477.7 0.0 copy-done.2
  477.7 0.0 copy-done.4
  477.7 0.0 copy-done.5
  477.7 1.4 divide_subtract_fusion.1
  479.1 152.0 %reduce-scatter.9.cloned.1.call-done = f32[16,512]{1,0:T(8,128)} async-done(((f32[1024,512]{1,0:T(8,128)}), f32[16,512]{1,0:T(8,128)}) %reduce-scatter.9.cloned.1.call-update) | async-done | bytes 32784 | tf_op jit(solution)/shard_map/reduce_scatter | solution.py:56
  631.2 0.0 copy-done.3
  631.2 0.0 copy-done.6
  631.2 0.0 copy-done.7
  631.2 1.4 divide_subtract_fusion
Async XLA Ops:
  7.2 93.7 %all-gather.11.cloned.1.call-start = ((), (), s32[]{:S(2)}) async-start(), calls=%async_computation.6 | async-start | bytes 2129920 | tf_op jit(solution)/shard_map/all_gather | solution.py:39
  7.9 137.3 %all-gather.5.cloned.1.call-start = ((), (), s32[]{:S(2)}) async-start(), calls=%async_computation.3 | async-start | bytes 1179648 | tf_op jit(solution)/shard_map/all_gather | solution.py:37
  8.6 225.8 %all-gather.7.cloned.1.call-start = ((), (), s32[]{:S(2)}) async-start(), calls=%async_computation.4 | async-start | bytes 2129920 | tf_op jit(solution)/shard_map/all_gather | solution.py:41
  9.4 310.0 %all-gather.9.cloned.1.call-start = ((), (), s32[]{:S(2)}) async-start(), calls=%async_computation.5 | async-start | bytes 2129920 | tf_op jit(solution)/shard_map/all_gather | solution.py:40
  10.0 467.7 %reduce-scatter.7.cloned.1.call-start = ((), (), s32[]{:S(2)}) async-start(), calls=%async_computation.7 | async-start | bytes 2129920 | tf_op jit(solution)/shard_map/reduce_scatter | solution.py:55
  104.4 214.9 %copy-start = (f32[256,512]{1,0:T(8,128)}, f32[256,512]{1,0:T(8,128)S(1)}, u32[]{:S(2)}) copy-start(f32[256,512]{1,0:T(8,128)S(1)} %fusion.11) | copy-start | bytes 1572868
  238.3 81.0 %copy-start.1 = (f32[256,512]{1,0:T(8,128)}, f32[256,512]{1,0:T(8,128)S(1)}, u32[]{:S(2)}) copy-start(f32[256,512]{1,0:T(8,128)S(1)} %fusion.10) | copy-start | bytes 1572868
  328.4 302.7 %reduce-scatter.9.cloned.1.call-start = ((), (), s32[]{:S(2)}) async-start(), calls=%async_computation.8 | async-start | bytes 2129920 | tf_op jit(solution)/shard_map/reduce_scatter | solution.py:56
  335.2 142.5 %copy-start.2 = (f32[16,512]{1,0:T(8,128)S(1)}, f32[16,512]{1,0:T(8,128)}, u32[]{:S(2)}) copy-start(f32[16,512]{1,0:T(8,128)} %param.11) | copy-start | bytes 98308
  335.2 142.5 %copy-start.4 = (f32[16,512]{1,0:T(8,128)S(1)}, f32[16,512]{1,0:T(8,128)}, u32[]{:S(2)}) copy-start(f32[16,512]{1,0:T(8,128)} %param.14) | copy-start | bytes 98308
  335.2 142.5 %copy-start.5 = (f32[16,512]{1,0:T(8,128)S(1)}, f32[16,512]{1,0:T(8,128)}, u32[]{:S(2)}) copy-start(f32[16,512]{1,0:T(8,128)} %param.15) | copy-start | bytes 98308
  335.2 296.0 %copy-start.3 = (f32[16,512]{1,0:T(8,128)S(1)}, f32[16,512]{1,0:T(8,128)}, u32[]{:S(2)}) copy-start(f32[16,512]{1,0:T(8,128)} %param.12) | copy-start | bytes 98308
  335.2 296.0 %copy-start.6 = (f32[16,512]{1,0:T(8,128)S(1)}, f32[16,512]{1,0:T(8,128)}, u32[]{:S(2)}) copy-start(f32[16,512]{1,0:T(8,128)} %param.16) | copy-start | bytes 98308
  335.2 296.0 %copy-start.7 = (f32[16,512]{1,0:T(8,128)S(1)}, f32[16,512]{1,0:T(8,128)}, u32[]{:S(2)}) copy-start(f32[16,512]{1,0:T(8,128)} %param.17) | copy-start | bytes 98308
Sparse Core Ops, SparseCore 0:
  11.3 89.5 all-gather.10
  102.9 42.1 all-gather.4
  148.5 85.9 all-gather.6
  237.6 81.6 all-gather.8
  328.5 149.1 reduce-scatter.6
  482.2 148.9 reduce-scatter.8
